TPU v7x, 512 devices: a whole 4x4x16 slice. The times are simulated.
512 devices in a mesh: row: 16 (over x, z_hi), col: 32 (over z_lo, y, core).
Axes of the slice: x: 4, y: 4, z: 16 (z_hi: 4, z_lo: 4; z = z_hi * 4 + z_lo), core: 2. Of those that a mesh axis runs over, the one named last changes fastest.
Arguments:
- i_list: int32 [2], replicated, may hold values from 0 to 127
- pairs: int32 [2, 2], replicated, may hold values from 0 to 127
- vir_offsets: int32 [2], replicated, may hold values from 0 to 960, as said below
- occ_energy: float32 [128], replicated, may hold values from -2 to -0.5
- vir_energy: float32 [1024], replicated, may hold values from 0.5 to 5
- amplitudes: bfloat16 [2, 1024, 1024], P(None, 'row', 'col'), may hold values from -6 to 6
- integrals: bfloat16 [2, 1024, 64, 128], P(None, 'row', 'col'), may hold values from -1.75 to 1.75
Outputs:
- density: bfloat16 [2, 1024, 64, 128], P(None, 'row', 'col')
- amp_grad: bfloat16 [2, 1024, 1024], P(None, 'row', 'col')
Inputs may be any that keep to these rules, and one draw needn't show every extreme that they name: `vir_offsets`: the first entry is a multiple of 128 and at most 896; the second is at most 960.
All inputs are finite; a program needn't handle non-finite values.
Results may differ from a plain program's by a relative error of at most 0.012.
Values may be sent and summed in bfloat16 or wider, within the bound.
A program may use at most 64 MiB of HBM per device.

v0:
```python
import jax
import jax.numpy as jnp
from jax import lax
from jax.sharding import PartitionSpec as P


def pick_energy(index_values, energies):
    table = jnp.arange(energies.shape[0], dtype=jnp.int32)
    onehot = (index_values[..., None] == table).astype(jnp.float32)
    return jnp.sum(onehot * energies, axis=-1)


def local(i_list, pairs, vir_offsets, occ_energy, vir_energy, amplitudes, integrals):
    n_pair = amplitudes.shape[0]
    block_c = amplitudes.shape[1]
    width = vir_energy.shape[0]
    n_i = integrals.shape[0]
    block_d = integrals.shape[1]
    width_b = integrals.shape[2]
    width_a = integrals.shape[3]
    tile = width_b * width_a
    row_pos = lax.axis_index("row")
    col_pos = lax.axis_index("col")
    amp_full = lax.all_gather(amplitudes, "col", axis=2, tiled=True)
    amp_rows = amp_full.reshape(n_pair * block_c, width)
    occ_sum = (
        pick_energy(i_list, occ_energy)[:, None]
        + pick_energy(pairs[:, 0], occ_energy)[None, :]
        + pick_energy(pairs[:, 1], occ_energy)[None, :]
    )
    e_c = lax.dynamic_slice_in_dim(vir_energy, row_pos * block_c, block_c)
    e_b = lax.dynamic_slice_in_dim(vir_energy, vir_offsets[1] + col_pos * width_b, width_b)
    e_a = lax.dynamic_slice_in_dim(vir_energy, vir_offsets[0], width_a)
    base = -(e_c[:, None, None] + e_b[None, :, None] + e_a[None, None, :]).reshape(block_c, tile)
    grad_sum = jnp.zeros((n_pair, block_c, width), jnp.float32)
    dens_list = []
    for slot in range(n_i):
        ints_full = lax.all_gather(integrals[slot], "row", axis=0, tiled=True).reshape(width, tile)
        triples = jnp.einsum("pcd,dx->pcx", amp_full, ints_full, preferred_element_type=jnp.float32)
        scaled = (triples / (occ_sum[slot][:, None, None] + base[None])).astype(jnp.bfloat16)
        z_rows = scaled.reshape(n_pair * block_c, tile)
        dens_part = lax.psum_scatter(
            lax.dot_general(
                amp_rows, z_rows, (((0,), (0,)), ((), ())), preferred_element_type=jnp.float32
            ).astype(jnp.bfloat16),
            "row",
            scatter_dimension=0,
            tiled=True,
        )
        dens_list.append(dens_part.reshape(block_d, width_b, width_a))
        grad_sum = grad_sum + jnp.einsum(
            "pcx,dx->pcd", scaled, ints_full, preferred_element_type=jnp.float32
        )
    density = jnp.stack(dens_list)
    amp_grad = lax.psum_scatter(grad_sum, "col", scatter_dimension=2, tiled=True).astype(
        jnp.bfloat16
    )
    return (density, amp_grad)


def solution(mesh):
    return jax.shard_map(
        local,
        mesh=mesh,
        in_specs=(P(), P(), P(), P(), P(), P(None, "row", "col"), P(None, "row", "col", None)),
        out_specs=(P(None, "row", "col", None), P(None, "row", "col")),
        check_vma=False,
    )
```

profile of v0, /device:TPU:1, one launch (start us, length us, event | category | flops | bytes accessed | tf_op | source)
XLA Modules:
  0.0 493.8 jit_solution(15006013021836459264)
XLA Ops:
  7.2 0.6 copy-done.3
  7.8 0.6 fusion.10
  10.4 47.4 %all_gather.9 = bf16[2,64,1024]{1,2,0:T(8,128)(2,1)S(1)} all-gather(bf16[2,64,32]{1,2,0:T(8,128)(2,1)S(1)} %copy-done.1), channel_id=1, replica_groups=mesh['row'=16,'col'=32] {'col'}, dimensions={2}, use_global_device_ids=true | all-gather | bytes 270336 | tf_op jit(solution)/shard_map/all_gather | solution.py:24
  57.8 54.0 %all-gather.1 = bf16[1,1024,2,128]{3,2,0,1:T(2,128)(2,1)S(1)} all-gather(bf16[1,64,2,128]{3,2,0,1:T(2,128)(2,1)S(1)} %get-tuple-element.8), channel_id=3, replica_groups=mesh['row'=16,'col'=32] {'row'}, dimensions={1}, use_global_device_ids=true | all-gather | bytes 557056 | tf_op jit(solution)/shard_map/all_gather | solution.py:38
  111.8 0.3 reshape.87
  112.1 0.3 copy-done.2
  112.5 0.2 slice_reduce_fusion.1
  112.7 0.6 copy-done.4
  113.3 0.2 fusion.7
  113.6 0.8 dynamic_slice.10
  114.4 0.8 dynamic_slice.9
  115.8 0.8 dynamic_slice.11
  116.7 0.1 add.125
  116.8 0.3 fusion.5
  117.1 0.3 fusion.2
  117.5 1.0 copy.21
  118.6 46.3 %all-gather = bf16[1,1024,2,128]{3,2,0,1:T(2,128)(2,1)S(1)} all-gather(bf16[1,64,2,128]{3,2,0,1:T(2,128)(2,1)S(1)} %get-tuple-element.7), channel_id=2, replica_groups=mesh['row'=16,'col'=32] {'row'}, dimensions={1}, use_global_device_ids=true | all-gather | bytes 557056 | tf_op jit(solution)/shard_map/all_gather | solution.py:38
  164.9 0.3 reshape.85
  165.2 0.3 fusion.4
  165.5 0.3 fusion.3
  165.9 1.0 copy.19
  167.0 0.3 fusion.11
  167.3 1.3 convolution_add_fusion
  168.6 61.5 %reduce-scatter.12.cloned.1.call-done = bf16[64,256]{1,0:T(8,128)(2,1)} async-done(((bf16[1024,256]{1,0:T(8,128)(2,1)}), bf16[64,256]{1,0:T(8,128)(2,1)}) %reduce-scatter.12.cloned.1.call-update) | async-done | bytes 32784
  230.1 0.9 copy.22
  231.0 0.1 copy.18
  231.1 110.2 %reduce-scatter.10.cloned.1.call-done = bf16[64,256]{1,0:T(8,128)(2,1)} async-done(((bf16[1024,256]{1,0:T(8,128)(2,1)}), bf16[64,256]{1,0:T(8,128)(2,1)}) %reduce-scatter.10.cloned.1.call-update) | async-done | bytes 32784
  341.3 0.9 copy.20
  342.2 0.1 copy.17
  342.3 0.7 pad_maximum_fusion
  343.0 142.9 %reduce-scatter.8.cloned.1.call-done = f32[2,64,32]{1,2,0:T(8,128)} async-done(((f32[2,64,1024]{1,2,0:T(8,128)}), f32[2,64,32]{1,2,0:T(8,128)}) %reduce-scatter.8.cloned.1.call-update) | async-done | bytes 16400 | tf_op jit(solution)/shard_map/reduce_scatter | solution.py:55
  485.9 1.4 convert_element_type.30
  (21 shorter events, 0.4 us)
Async XLA Ops:
  7.2 0.7 copy-start.3
  7.2 222.9 %reduce-scatter.12.cloned.1.call-start = ((), (), s32[]{:S(2)}) async-start(), calls=%async_computation.5 | async-start | bytes 557056
  8.4 2.0 copy-start.1
  10.4 47.4 %copy-start = (bf16[2,64,2,128]{3,2,1,0:T(2,128)(2,1)S(1)}, bf16[2,64,2,128]{3,2,1,0:T(2,128)(2,1)}, u32[]{:S(2)}) copy-start(bf16[2,64,2,128]{3,2,1,0:T(2,128)(2,1)} %param.13) | copy-start | bytes 196612
  111.8 0.7 copy-start.2
  112.7 0.7 copy-start.4
  112.7 0.7 copy-start.5
  118.5 222.8 %reduce-scatter.10.cloned.1.call-start = ((), (), s32[]{:S(2)}) async-start(), calls=%async_computation.4 | async-start | bytes 557056
  166.9 318.9 %reduce-scatter.8.cloned.1.call-start = ((), (), s32[]{:S(2)}) async-start(), calls=%async_computation.3 | async-start | bytes 1081344 | tf_op jit(solution)/shard_map/reduce_scatter | solution.py:55
Sparse Core Ops, SparseCore 0:
  118.7 111.3 reduce-scatter.11
  234.7 106.5 reduce-scatter.9
  344.1 141.7 reduce-scatter.7
where the time goes:
time: 498 us; the launch traced here: 494 us
  waiting for transfers between devices  315 us (63%)
  blocking collectives  148 us (30%)
  between operations  16.5 us (3%)
  local copies, waits for them, and re-layouts  9.5 us (2%)
    unnamed x5, waiting for transfers between devices  172 us
    reduce_scatter x1, waiting for transfers between devices, local(): lax.psum_scatter(grad_sum, 'col', scatter_dimension=2, tiled=True)  143 us
    all_gather x2, blocking collectives, local(): lax.all_gather(integrals[slot], 'row', axis=0, tiled=True)  100 us
    all_gather x1, blocking collectives, local(): amp_full = lax.all_gather(amplitudes, 'col', axis=2, tiled=True)  47.4 us
  transfers between devices with their start and end apart: 3, of which 3 were waited for; matrix products, arithmetic and copies ran while one was open for 1% of the time, Pallas kernels for 0%

commit v1 on v0

v1 whole, which is shorter than its diff:
```python
import jax
import jax.numpy as jnp
from jax import lax
from jax.experimental import pallas as pl
from jax.experimental.pallas import tpu as pltpu
from jax.sharding import PartitionSpec as P

BF16 = jnp.bfloat16
F32 = jnp.float32
MESH = pl.DeviceIdType.MESH


def pick_energy(index_values, energies):
    table = jnp.arange(energies.shape[0], dtype=jnp.int32)
    onehot = (index_values[..., None] == table).astype(jnp.float32)
    return jnp.sum(onehot * energies, axis=-1)


def kernel(
    amp_in, int_in, row_ref, ea_ref, dens_out, grad_out,
    amp, ints, scaled, grad, grad_core, grad_y, grad_yrecv, grad_z, grad_zrecv,
    dens, dens_xrecv, dens_sum, dens_zrecv,
    az_s, az_r, ay_s, ay_r, ac_s, ac_r, iz_s, iz_r, ix_s, ix_r,
    dx_s, dx_r, dz_s, dz_r, gc_s, gc_r, gy_s, gy_r, gz_s, gz_r,
):
    row = lax.axis_index("row")
    col = lax.axis_index("col")
    x, zh = row // 4, row % 4
    zl, y, core = col // 8, (col // 2) % 4, col % 2
    z = zh * 4 + zl

    def z_peer(o):
        t = (z + o) % 16
        return (x * 4 + t // 4, (t % 4) * 8 + y * 2 + core)

    def zh_peer(k):
        return (x * 4 + (zh + k) % 4, col)

    def x_peer(j):
        return (((x + j) % 4) * 4 + zh, col)

    def y_peer(j):
        return (row, zl * 8 + ((y + j) % 4) * 2 + core)

    core_peer = (row, col + 1 - 2 * core)

    def remote(src, dst, ssem, rsem, dev):
        return pltpu.make_async_remote_copy(
            src_ref=src, dst_ref=dst, send_sem=ssem, recv_sem=rsem,
            device_id=dev, device_id_type=MESH,
        )

    barrier = pltpu.get_barrier_semaphore()

    def greet(dev):
        pl.semaphore_signal(barrier, inc=1, device_id=dev, device_id_type=MESH)

    @pl.loop(1, 16)
    def _(o):
        greet(z_peer(o))

    for j in range(1, 4):
        greet(x_peer(j))
        greet(y_peer(j))
    greet(core_peer)
    pl.semaphore_wait(barrier, 22)

    def amp_z(o):
        return remote(amp_in, amp.at[zh, zl, y, core], az_s.at[o], az_r.at[o], z_peer(o))

    @pl.loop(1, 16)
    def _(k):
        o = (8 + ((k + 0) // 2) * (2 * (k % 2) - 1) + 16) % 16
        amp_z(o).start()

    def int_z(k):
        return remote(int_in.at[(zh + k) % 4], ints.at[row], iz_s.at[k], iz_r.at[k], zh_peer(k))

    for k in (2, 1, 3):
        int_z(k).start()

    amp[zh, zl, y, core] = amp_in[...]
    ints[row] = int_in[zh]

    def amp_piece(o):
        s = (z - o + 16) % 16
        return s // 4, s % 4

    def amp_y(o, j):
        h, l = amp_piece(o)
        block = amp.at[h, l, y, core]
        return remote(block, block, ay_s.at[o, j], ay_r.at[o, j], y_peer(j))

    def amp_y_own(j):
        return remote(amp_in, amp.at[zh, zl, y, core], ay_s.at[0, j], ay_r.at[0, j], y_peer(j))

    def amp_c(o):
        h, l = amp_piece(o)
        block = amp.at[h, l, :, core]
        return remote(block, block, ac_s.at[o], ac_r.at[o], core_peer)

    def int_x(k, j):
        block = ints.at[x * 4 + (zh - k + 4) % 4]
        src = int_in.at[zh] if k == 0 else block
        return remote(src, block, ix_s.at[k, j], ix_r.at[k, j], x_peer(j))

    for j in (2, 1, 3):
        amp_y_own(j).start()
        int_x(0, j).start()

    @pl.loop(1, 16)
    def _(k):
        o = ((k // 2) * (1 - 2 * (k % 2)) - (k % 2) + 16) % 16
        amp_z(o).wait_recv()
        for j in (2, 1, 3):
            amp_y(o, j).start()

    for k in (1, 3, 2):
        int_z(k).wait_recv()
        for j in (2, 1, 3):
            int_x(k, j).start()

    for j in (1, 2, 3):
        amp_y_own(j).wait_recv()
    amp_c(0).start()

    @pl.loop(1, 16)
    def _(k):
        o = ((k // 2) * (1 - 2 * (k % 2)) - (k % 2) + 16) % 16
        for j in (1, 2, 3):
            amp_y(o, j).wait_recv()
        amp_c(o).start()

    for k in (0, 1, 3, 2):
        for j in (1, 2, 3):
            int_x(k, j).wait_recv()
    ints_all = ints[...].reshape(1024, 128)
    ints_t = ints_all.T

    @pl.loop(0, 16)
    def _(o):
        amp_c(o).wait_recv()

    for h in range(4):
        t = jnp.dot(ints_t, amp[h].reshape(1024, 128), preferred_element_type=F32)
        scaled[h] = (t / (row_ref[h] - ea_ref[...])).astype(BF16)

    def grad_c(h):
        return remote(
            grad.at[h, :, :, 1 - core], grad_core.at[h], gc_s.at[h], gc_r.at[h], core_peer
        )

    for k in (2, 1, 3, 0):
        h = (zh + k) % 4
        g = jnp.dot(ints_all, scaled[h], preferred_element_type=F32)
        grad[h] = g.astype(BF16).reshape(4, 4, 2, 32, 128)
        grad_c(h).start()

    def dens_x(j):
        return remote(
            dens.at[(x + j) % 4], dens_xrecv.at[j], dx_s.at[j], dx_r.at[j], x_peer(j)
        )

    for j in (2, 1, 3, 0):
        t = (x + j) % 4
        acc = jnp.zeros((256, 128), F32)
        for h in range(4):
            acc += lax.dot_general(
                amp[h, t].reshape(256, 128), scaled[h], (((1,), (1,)), ((), ())),
                preferred_element_type=F32,
            )
        dens[t] = acc.astype(BF16).reshape(4, 64, 128)
        if j:
            dens_x(j).start()

    def grad_yc(k, j):
        h = (zh + k) % 4
        return remote(
            grad_y.at[h, :, (y + j) % 4], grad_yrecv.at[k, j], gy_s.at[k, j], gy_r.at[k, j],
            y_peer(j),
        )

    for k in (2, 1, 3, 0):
        h = (zh + k) % 4
        grad_c(h).wait_recv()
        s = grad[h, :, :, core].astype(F32) + grad_core[h].astype(F32)
        grad_y[h] = s.astype(BF16)
        for j in (2, 1, 3):
            grad_yc(k, j).start()

    def dens_z(k):
        return remote(
            dens_sum.at[(zh + k) % 4], dens_zrecv.at[k], dz_s.at[k], dz_r.at[k], zh_peer(k)
        )

    total = dens[x].astype(F32)
    for j in (1, 3, 2):
        dens_x(j).wait_recv()
        total += dens_xrecv[j].astype(F32)
    dens_sum[...] = total.astype(BF16)
    for k in (2, 1, 3):
        dens_z(k).start()

    def grad_zc(k, m):
        t = (zl + m) % 4
        o = (4 * k + t - zl + 16) % 16
        return remote(
            grad_z.at[(zh + k) % 4, t], grad_zrecv.at[o], gz_s.at[o], gz_r.at[o], z_peer(o)
        )

    for k in (2, 1, 3, 0):
        h = (zh + k) % 4
        s = grad_y[h, :, y].astype(F32)
        for j in (1, 3, 2):
            grad_yc(k, j).wait_recv()
            s += grad_yrecv[k, j].astype(F32)
        grad_z[h] = s.astype(BF16)
        for m in range(4):
            if k or m:
                grad_zc(k, m).start()

    dens_out[zh] = dens_sum[zh]
    for k in (1, 3, 2):
        dens_z(k).wait_recv()
        dens_out[(zh - k + 4) % 4] = dens_zrecv[k]

    def grad_zo(o):
        return remote(
            grad_z.at[0, 0], grad_zrecv.at[o], gz_s.at[o], gz_r.at[o], z_peer(o)
        )

    def add_z(o, s):
        grad_zo(o).wait_recv()
        return s + grad_zrecv[o].astype(F32)

    s = lax.fori_loop(1, 16, add_z, grad_z[zh, zl].astype(F32))
    grad_out[...] = s.T.astype(BF16)

    @pl.loop(1, 16)
    def _(o):
        amp_z(o).wait_send()
        grad_zo(o).wait_send()

    @pl.loop(0, 16)
    def _(o):
        for j in (1, 2, 3):
            amp_y(o, j).wait_send()
        amp_c(o).wait_send()

    for k in range(4):
        for j in (1, 2, 3):
            int_x(k, j).wait_send()
            grad_yc(k, j).wait_send()
        grad_c(k).wait_send()
    for k in (1, 2, 3):
        int_z(k).wait_send()
        dens_x(k).wait_send()
        dens_z(k).wait_send()


def local(i_list, pairs, vir_offsets, occ_energy, vir_energy, amplitudes, integrals):
    row = lax.axis_index("row")
    col = lax.axis_index("col")
    x, zh = row // 4, row % 4
    occ = (
        pick_energy(i_list, occ_energy)[:, None]
        + pick_energy(pairs[:, 0], occ_energy)[None, :]
        + pick_energy(pairs[:, 1], occ_energy)[None, :]
    )
    occ = jnp.where(zh // 2 == 0, occ[0], occ[1])
    e_c = lax.dynamic_slice_in_dim(vir_energy, x * 256, 256).reshape(4, 1, 64)
    e_b = lax.dynamic_slice_in_dim(vir_energy, vir_offsets[1] + col * 2 + zh % 2, 1)
    e_a = lax.dynamic_slice_in_dim(vir_energy, vir_offsets[0], 128)
    row_part = (occ[None, :, None] - (e_c + e_b[0])).reshape(4, 1, 128)
    e_a = jnp.broadcast_to(e_a[:, None], (128, 128))
    amp_t = amplitudes.transpose(2, 0, 1).reshape(32, 128)
    ints_t = integrals.transpose(0, 2, 1, 3).reshape(4, 64, 128)
    vmem = pl.BlockSpec(memory_space=pltpu.VMEM)
    dma = pltpu.SemaphoreType.DMA
    dens, grad = pl.pallas_call(
        kernel,
        out_shape=(
            jax.ShapeDtypeStruct((4, 64, 128), BF16),
            jax.ShapeDtypeStruct((128, 32), BF16),
        ),
        in_specs=[vmem] * 4,
        out_specs=(vmem, vmem),
        scratch_shapes=[
            pltpu.VMEM((4, 4, 4, 2, 32, 128), BF16),
            pltpu.VMEM((16, 64, 128), BF16),
            pltpu.VMEM((4, 128, 128), BF16),
            pltpu.VMEM((4, 4, 4, 2, 32, 128), BF16),
            pltpu.VMEM((4, 4, 4, 32, 128), BF16),
            pltpu.VMEM((4, 4, 4, 32, 128), BF16),
            pltpu.VMEM((4, 4, 4, 32, 128), BF16),
            pltpu.VMEM((4, 4, 32, 128), BF16),
            pltpu.VMEM((16, 32, 128), BF16),
            pltpu.VMEM((4, 4, 64, 128), BF16),
            pltpu.VMEM((4, 4, 64, 128), BF16),
            pltpu.VMEM((4, 64, 128), BF16),
            pltpu.VMEM((4, 64, 128), BF16),
            dma((16,)), dma((16,)), dma((16, 4)), dma((16, 4)), dma((16,)), dma((16,)),
            dma((4,)), dma((4,)), dma((4, 4)), dma((4, 4)),
            dma((4,)), dma((4,)), dma((4,)), dma((4,)),
            dma((4,)), dma((4,)), dma((4, 4)), dma((4, 4)), dma((16,)), dma((16,)),
        ],
        compiler_params=pltpu.CompilerParams(collective_id=0, has_side_effects=True),
    )(amp_t, ints_t, row_part, e_a)
    density = dens.reshape(2, 2, 64, 128).transpose(0, 2, 1, 3)
    return density, grad.reshape(2, 64, 32)


def solution(mesh):
    return jax.shard_map(
        local,
        mesh=mesh,
        in_specs=(P(), P(), P(), P(), P(), P(None, "row", "col"), P(None, "row", "col", None)),
        out_specs=(P(None, "row", "col", None), P(None, "row", "col")),
        check_vma=False,
    )
```

time: 498 us -> 70.3 us (0.14)
  waiting for transfers between devices: 315 us -> 0 us
  blocking collectives: 148 us -> 0 us
  Pallas kernels: 0 us -> 56.3 us
  between operations: 16.5 us -> 3.37 us
    unnamed x5 -> x0, waiting for transfers between devices: 172 us -> none
    all_gather x3 -> x0, blocking collectives: 148 us -> none  [the longest x2 100 us: local(): lax.all_gather(integrals[slot], 'row', axis=0, tiled=True)]
    reduce_scatter x1 -> x0, waiting for transfers between devices: 143 us -> none  [local(): lax.psum_scatter(grad_sum, 'col', scatter_dimension=2, tiled=True)]
    pallas_call x0 -> x1, Pallas kernels: none -> 56.3 us  [local(): pl.pallas_call(kernel, out_shape=(jax.ShapeDtypeStruct((4, 64, 128), BF16...]
  transfers between devices with their start and end apart: 3 -> 0, of which waited for: 3 -> 0; matrix products, arithmetic and copies ran while one was open for 1% -> 0% of each run, Pallas kernels for 0% -> 0%
where the time goes in v1:
time: 70.3 us; the launch traced here: 69.9 us
  Pallas kernels  56.3 us (80%)
  local copies, waits for them, and re-layouts  8.61 us (12%)
  between operations  3.37 us (5%)
  other arithmetic  1.58 us (2%)
    pallas_call x1, Pallas kernels, local(): pl.pallas_call(kernel, out_shape=(jax.ShapeDtypeStruct((4, 64, 128), BF16...  56.3 us
    unnamed x17, local copies, waits for them, and re-layouts  3.29 us
    reshape x1, local copies, waits for them, and re-layouts, local(): density = dens.reshape(2, 2, 64, 128).transpose(0, 2, 1, 3)  1.54 us

profile of v1, /device:TPU:1, one launch (start us, length us, event | category | flops | bytes accessed | tf_op | source)
XLA Modules:
  0.0 69.9 jit_solution(851409119739081960)
XLA Ops:
  0.7 0.0 copy-start.3
  0.7 0.7 copy-done.3
  1.4 0.2 slice_reduce_fusion.1
  1.5 0.0 copy-start.5
  1.6 0.0 copy-start.6
  1.6 0.6 copy-done.5
  2.2 0.0 copy-done.6
  2.2 0.2 fusion
  2.4 0.1 add_add_fusion
  2.5 0.1 sub.34
  2.6 0.0 copy-start.4
  2.6 0.1 sub.35
  2.7 0.6 copy-done.4
  3.3 0.6 fusion.4
  4.5 0.0 copy-start.7
  4.5 0.7 copy-done.7
  5.2 0.6 dynamic_slice.10
  7.7 0.1 dynamic_slice.11
  7.8 0.7 %dynamic-slice_add_fusion = f32[256]{0:T(256)S(1)} fusion(f32[1024]{0:T(1024)S(1)} %copy-done.7, s32[]{:T(128)S(6)} %select_n.48, f32[]{:T(128)} %bitcast.5), kind=kLoop, calls=%fused_computation.7 | loop fusion | flops 256 | bytes 2056 | tf_op jit(solution)/shard_map/add | solution.py:274
  8.5 0.1 add.72
  8.6 0.1 sub.39
  8.7 0.6 broadcast_subtract_fusion.row_ref
  9.3 0.0 copy-done.2
  9.3 0.7 reshape.78.amp_in
  10.0 0.7 %broadcast_in_dim.2.ea_ref = f32[128,128]{1,0:T(8,128)} broadcast(f32[128]{0:T(128)S(1)} %dynamic_slice.11), dimensions={0} | broadcast | bytes 66048 | tf_op jit(solution)/shard_map/broadcast_in_dim | solution.py:275
  10.7 0.0 copy-done
  10.7 0.6 copy.14
  11.3 56.3 %shard_map.86 = (bf16[4,64,128]{2,1,0:T(8,128)(2,1)}, bf16[128,32]{1,0:T(8,128)(2,1)}) custom-call(bf16[32,128]{1,0:T(8,128)(2,1)} %reshape.78.amp_in, bf16[4,64,128]{2,1,0:T(8,128)(2,1)} %bitcast.13, f32[4,1,128]{2,1,0:T(1,128)} %broadcast_subtract_fusion.row_ref, f32[128,128]{1,0:T(8,128)} %broadcast_in_dim.2.ea_ref), custom_call_target="tpu_custom_call" | custom-call | tf_op jit(solution)/shard_map/pallas_call | solution.py:280
  67.6 0.0 copy-start.1
  67.7 1.5 %copy.18 = bf16[2,2,64,128]{3,1,2,0:T(2,128)(2,1)} copy(bf16[2,2,64,128]{3,2,1,0:T(8,128)(2,1)} %bitcast.16) | data formatting | bytes 131072 | tf_op jit(solution)/shard_map/reshape | solution.py:309
  69.2 0.0 copy-done.1
  69.2 0.7 copy.16
  (5 shorter events, 0.0 us)
Async XLA Ops:
  0.7 0.7 copy-start.3
  1.5 0.7 copy-start.5
  1.6 0.7 copy-start.6
  2.6 0.7 copy-start.4
  4.5 0.7 copy-start.7
  5.8 3.5 %copy-start.2 = (bf16[2,64,32]{1,2,0:T(8,128)(2,1)S(1)}, bf16[2,64,32]{1,2,0:T(8,128)(2,1)}, u32[]{:S(2)}) copy-start(bf16[2,64,32]{1,2,0:T(8,128)(2,1)} %param.12) | copy-start | bytes 24580
  8.6 2.1 %copy-start = (bf16[2,64,2,128]{3,2,1,0:T(2,128)(2,1)S(1)}, bf16[2,64,2,128]{3,2,1,0:T(2,128)(2,1)}, u32[]{:S(2)}) copy-start(bf16[2,64,2,128]{3,2,1,0:T(2,128)(2,1)} %param.13) | copy-start | bytes 196612
  67.6 1.6 %copy-start.1 = (bf16[128,32]{1,0:T(8,128)(2,1)S(1)}, bf16[128,32]{1,0:T(8,128)(2,1)}, u32[]{:S(2)}) copy-start(bf16[128,32]{1,0:T(8,128)(2,1)} %get-tuple-element.5) | copy-start | bytes 24580

commit v2 on v1

--- a/solution.py
+++ b/solution.py
@@ -10,14 +10,10 @@
 MESH = pl.DeviceIdType.MESH
 
 
-def pick_energy(index_values, energies):
-    table = jnp.arange(energies.shape[0], dtype=jnp.int32)
-    onehot = (index_values[..., None] == table).astype(jnp.float32)
-    return jnp.sum(onehot * energies, axis=-1)
-
-
 def kernel(
-    amp_in, int_in, row_ref, ea_ref, dens_out, grad_out,
+    i_list, pairs, vir_offsets, occ_energy, vir_energy, vir_rows, amp_hbm, int_hbm,
+    dens_out, grad_out,
+    i_sm, pairs_sm, off_sm, occ_sm, vir_sm, vir_vm, amp_vm, int_vm, amp_in, int_in, in_sem,
     amp, ints, scaled, grad, grad_core, grad_y, grad_yrecv, grad_z, grad_zrecv,
     dens, dens_xrecv, dens_sum, dens_zrecv,
     az_s, az_r, ay_s, ay_r, ac_s, ac_r, iz_s, iz_r, ix_s, ix_r,
@@ -50,6 +46,16 @@
             device_id=dev, device_id_type=MESH,
         )
 
+    loads = [
+        pltpu.make_async_copy(src, dst, in_sem.at[n])
+        for n, (src, dst) in enumerate((
+            (amp_hbm, amp_vm), (int_hbm, int_vm), (vir_rows, vir_vm), (i_list, i_sm),
+            (pairs, pairs_sm), (vir_offsets, off_sm), (occ_energy, occ_sm), (vir_energy, vir_sm),
+        ))
+    ]
+    for load in loads:
+        load.start()
+
     barrier = pltpu.get_barrier_semaphore()
 
     def greet(dev):
@@ -63,6 +69,9 @@
         greet(x_peer(j))
         greet(y_peer(j))
     greet(core_peer)
+    loads[0].wait()
+    amp_in[...] = jnp.concatenate([amp_vm[0], amp_vm[1]], axis=1)
+    amp[zh, zl, y, core] = amp_in[...]
     pl.semaphore_wait(barrier, 22)
 
     def amp_z(o):
@@ -73,13 +82,18 @@
         o = (8 + ((k + 0) // 2) * (2 * (k % 2) - 1) + 16) % 16
         amp_z(o).start()
 
+    loads[1].wait()
+    for i in range(2):
+        v = int_vm[i].astype(F32)
+        for b in range(2):
+            int_in[2 * i + b] = v[:, b, :].astype(BF16)
+
     def int_z(k):
         return remote(int_in.at[(zh + k) % 4], ints.at[row], iz_s.at[k], iz_r.at[k], zh_peer(k))
 
     for k in (2, 1, 3):
         int_z(k).start()
 
-    amp[zh, zl, y, core] = amp_in[...]
     ints[row] = int_in[zh]
 
     def amp_piece(o):
@@ -107,6 +121,22 @@
     for j in (2, 1, 3):
         amp_y_own(j).start()
         int_x(0, j).start()
+
+    for load in loads[2:]:
+        load.wait()
+    e_a = jnp.broadcast_to(vir_vm[pl.ds(off_sm[0] // 128, 1), :], (128, 128)).T
+    e_b = vir_sm[off_sm[1] + col * 2 + zh % 2]
+    e_i = occ_sm[i_sm[zh // 2]]
+    occ0 = e_i + occ_sm[pairs_sm[0, 0]] + occ_sm[pairs_sm[0, 1]]
+    occ1 = e_i + occ_sm[pairs_sm[1, 0]] + occ_sm[pairs_sm[1, 1]]
+    first = lax.broadcasted_iota(jnp.int32, (1, 128), 1) < 64
+    occ = jnp.where(first, occ0, occ1)
+    row_part = []
+    for h in range(4):
+        e_c = vir_vm[pl.ds(x * 2 + h // 2, 1), :]
+        turned = pltpu.roll(e_c, 64, axis=1)
+        e_c = jnp.where(first, turned, e_c) if h % 2 else jnp.where(first, e_c, turned)
+        row_part.append(occ - (e_c + e_b))
 
     @pl.loop(1, 16)
     def _(k):
@@ -143,7 +173,7 @@
 
     for h in range(4):
         t = jnp.dot(ints_t, amp[h].reshape(1024, 128), preferred_element_type=F32)
-        scaled[h] = (t / (row_ref[h] - ea_ref[...])).astype(BF16)
+        scaled[h] = (t / (row_part[h] - e_a)).astype(BF16)
 
     def grad_c(h):
         return remote(
@@ -234,7 +264,8 @@
         return s + grad_zrecv[o].astype(F32)
 
     s = lax.fori_loop(1, 16, add_z, grad_z[zh, zl].astype(F32))
-    grad_out[...] = s.T.astype(BF16)
+    grad_out[0] = s[:, :64].astype(BF16)
+    grad_out[1] = s[:, 64:].astype(BF16)
 
     @pl.loop(1, 16)
     def _(o):
@@ -259,33 +290,23 @@
 
 
 def local(i_list, pairs, vir_offsets, occ_energy, vir_energy, amplitudes, integrals):
-    row = lax.axis_index("row")
-    col = lax.axis_index("col")
-    x, zh = row // 4, row % 4
-    occ = (
-        pick_energy(i_list, occ_energy)[:, None]
-        + pick_energy(pairs[:, 0], occ_energy)[None, :]
-        + pick_energy(pairs[:, 1], occ_energy)[None, :]
-    )
-    occ = jnp.where(zh // 2 == 0, occ[0], occ[1])
-    e_c = lax.dynamic_slice_in_dim(vir_energy, x * 256, 256).reshape(4, 1, 64)
-    e_b = lax.dynamic_slice_in_dim(vir_energy, vir_offsets[1] + col * 2 + zh % 2, 1)
-    e_a = lax.dynamic_slice_in_dim(vir_energy, vir_offsets[0], 128)
-    row_part = (occ[None, :, None] - (e_c + e_b[0])).reshape(4, 1, 128)
-    e_a = jnp.broadcast_to(e_a[:, None], (128, 128))
-    amp_t = amplitudes.transpose(2, 0, 1).reshape(32, 128)
-    ints_t = integrals.transpose(0, 2, 1, 3).reshape(4, 64, 128)
+    hbm = pl.BlockSpec(memory_space=pltpu.HBM)
     vmem = pl.BlockSpec(memory_space=pltpu.VMEM)
     dma = pltpu.SemaphoreType.DMA
     dens, grad = pl.pallas_call(
         kernel,
         out_shape=(
             jax.ShapeDtypeStruct((4, 64, 128), BF16),
-            jax.ShapeDtypeStruct((128, 32), BF16),
+            jax.ShapeDtypeStruct((2, 32, 64), BF16),
         ),
-        in_specs=[vmem] * 4,
+        in_specs=[hbm] * 8,
         out_specs=(vmem, vmem),
         scratch_shapes=[
+            pltpu.SMEM((2,), jnp.int32), pltpu.SMEM((2, 2), jnp.int32),
+            pltpu.SMEM((2,), jnp.int32), pltpu.SMEM((128,), F32), pltpu.SMEM((1024,), F32),
+            pltpu.VMEM((8, 128), F32), pltpu.VMEM((2, 32, 64), BF16),
+            pltpu.VMEM((2, 64, 2, 128), BF16), pltpu.VMEM((32, 128), BF16),
+            pltpu.VMEM((4, 64, 128), BF16), dma((8,)),
             pltpu.VMEM((4, 4, 4, 2, 32, 128), BF16),
             pltpu.VMEM((16, 64, 128), BF16),
             pltpu.VMEM((4, 128, 128), BF16),
@@ -305,9 +326,12 @@
             dma((4,)), dma((4,)), dma((4, 4)), dma((4, 4)), dma((16,)), dma((16,)),
         ],
         compiler_params=pltpu.CompilerParams(collective_id=0, has_side_effects=True),
-    )(amp_t, ints_t, row_part, e_a)
+    )(
+        i_list, pairs, vir_offsets, occ_energy, vir_energy, vir_energy.reshape(8, 128),
+        amplitudes.transpose(0, 2, 1), integrals,
+    )
     density = dens.reshape(2, 2, 64, 128).transpose(0, 2, 1, 3)
-    return density, grad.reshape(2, 64, 32)
+    return density, grad.transpose(0, 2, 1)
 
 
 def solution(mesh):

time: 70.3 us -> 59.5 us (0.85)
  local copies, waits for them, and re-layouts: 8.61 us -> 2.15 us
  between operations: 3.37 us -> 0.65 us
  other arithmetic: 1.58 us -> 0 us
    unnamed x17 -> x3, local copies, waits for them, and re-layouts: 3.29 us -> 0.61 us
    add x2 -> x0, other arithmetic: 0.79 us -> none  [the longest x1 0.72 us: local(): row_part = (occ[None, :, None] - (e_c + e_b[0])).reshape(4, 1, 128)]
    slice x2 -> x0, local copies, waits for them, and re-layouts: 0.75 us -> none  [the longest x1 0.58 us: local(): e_a = lax.dynamic_slice_in_dim(vir_energy, vir_offsets[0], 128)]
where the time goes in v2:
time: 59.5 us; the launch traced here: 59.3 us
  Pallas kernels  56.5 us (95%)
  local copies, waits for them, and re-layouts  2.15 us (4%)
  between operations  0.65 us (1%)
    pallas_call x1, Pallas kernels, local(): pl.pallas_call(kernel, out_shape=(jax.ShapeDtypeStruct((4, 64, 128), BF16...  56.5 us
    reshape x1, local copies, waits for them, and re-layouts, local(): density = dens.reshape(2, 2, 64, 128).transpose(0, 2, 1, 3)  1.54 us

profile of v2, /device:TPU:1, one launch (start us, length us, event | category | flops | bytes accessed | tf_op | source)
XLA Modules:
  0.0 59.3 jit_solution(16892391468250060566)
XLA Ops:
  0.6 56.5 %shard_map.86 = (bf16[4,64,128]{2,1,0:T(8,128)(2,1)}, bf16[2,32,64]{2,1,0:T(8,128)(2,1)}) custom-call(s32[2]{0:T(128)} %i_list.1, s32[2,2]{1,0:T(2,128)} %pairs.1, s32[2]{0:T(128)} %vir_offsets.1, f32[128]{0:T(128)} %occ_energy.1, f32[1024]{0:T(1024)} %vir_energy.1, f32[8,128]{1,0:T(8,128)} %bitcast.9, bf16[2,32,64]{2,1,0:T(8,128)(2,1)} %bitcast.11, ...), custom_call_target="tpu_custom_call" | custom-call | tf_op jit(solution)/shard_map/pallas_call | solution.py:296
  57.1 0.0 copy-start
  57.1 1.5 %copy.11 = bf16[2,2,64,128]{3,1,2,0:T(2,128)(2,1)} copy(bf16[2,2,64,128]{3,2,1,0:T(8,128)(2,1)} %bitcast.8) | data formatting | bytes 131072 | tf_op jit(solution)/shard_map/reshape | solution.py:333
  58.7 0.0 copy-done
  58.7 0.6 %copy.13 = bf16[2,64,32]{1,2,0:T(8,128)(2,1)} copy(bf16[2,64,32]{1,2,0:T(8,128)(2,1)S(1)} %bitcast.10) | data formatting | bytes 16384
Async XLA Ops:
  57.1 1.6 %copy-start = (bf16[2,32,64]{2,1,0:T(8,128)(2,1)S(1)}, bf16[2,32,64]{2,1,0:T(8,128)(2,1)}, u32[]{:S(2)}) copy-start(bf16[2,32,64]{2,1,0:T(8,128)(2,1)} %get-tuple-element.5) | copy-start | bytes 24580

commit v3 on v2

--- a/solution.py
+++ b/solution.py
@@ -13,7 +13,7 @@
 def kernel(
     i_list, pairs, vir_offsets, occ_energy, vir_energy, vir_rows, amp_hbm, int_hbm,
     dens_out, grad_out,
-    i_sm, pairs_sm, off_sm, occ_sm, vir_sm, vir_vm, amp_vm, int_vm, amp_in, int_in, in_sem,
+    i_sm, pairs_sm, off_sm, occ_sm, vir_sm, vir_vm, amp_vm, int_vm, amp_in, int_in, in_sem, relay, ir_s, ir_r,
     amp, ints, scaled, grad, grad_core, grad_y, grad_yrecv, grad_z, grad_zrecv,
     dens, dens_xrecv, dens_sum, dens_zrecv,
     az_s, az_r, ay_s, ay_r, ac_s, ac_r, iz_s, iz_r, ix_s, ix_r,
@@ -61,10 +61,8 @@
     def greet(dev):
         pl.semaphore_signal(barrier, inc=1, device_id=dev, device_id_type=MESH)
 
-    @pl.loop(1, 16)
-    def _(o):
+    for o in (1, 2, 3, 4, 12, 13, 14, 15):
         greet(z_peer(o))
-
     for j in range(1, 4):
         greet(x_peer(j))
         greet(y_peer(j))
@@ -72,14 +70,12 @@
     loads[0].wait()
     amp_in[...] = jnp.concatenate([amp_vm[0], amp_vm[1]], axis=1)
     amp[zh, zl, y, core] = amp_in[...]
-    pl.semaphore_wait(barrier, 22)
+    pl.semaphore_wait(barrier, 15)
 
     def amp_z(o):
         return remote(amp_in, amp.at[zh, zl, y, core], az_s.at[o], az_r.at[o], z_peer(o))
 
-    @pl.loop(1, 16)
-    def _(k):
-        o = (8 + ((k + 0) // 2) * (2 * (k % 2) - 1) + 16) % 16
+    for o in (4, 12, 3, 13, 2, 14, 1, 15):
         amp_z(o).start()
 
     loads[1].wait()
@@ -91,7 +87,22 @@
     def int_z(k):
         return remote(int_in.at[(zh + k) % 4], ints.at[row], iz_s.at[k], iz_r.at[k], zh_peer(k))
 
-    for k in (2, 1, 3):
+    def int_relay(n):
+        return remote(
+            int_in.at[(zh + 2) % 4, pl.ds(32 * n, 32)], relay.at[n], ir_s.at[n], ir_r.at[n],
+            zh_peer(1 + 2 * n),
+        )
+
+    def int_onward(n):
+        k = 1 + 2 * n
+        return remote(
+            relay.at[n], ints.at[x * 4 + (zh + 4 - k) % 4, pl.ds(32 * n, 32)],
+            iz_s.at[2 - 2 * n], iz_r.at[2 - 2 * n], zh_peer(k),
+        )
+
+    for n in range(2):
+        int_relay(n).start()
+    for k in (1, 3):
         int_z(k).start()
 
     ints[row] = int_in[zh]
@@ -138,25 +149,53 @@
         e_c = jnp.where(first, turned, e_c) if h % 2 else jnp.where(first, e_c, turned)
         row_part.append(occ - (e_c + e_b))
 
-    @pl.loop(1, 16)
-    def _(k):
-        o = ((k // 2) * (1 - 2 * (k % 2)) - (k % 2) + 16) % 16
-        amp_z(o).wait_recv()
+    def amp_on(o):
+        near = 4 if o < 8 else 12
+        h, l = amp_piece(near)
+        block = amp.at[h, l, y, core]
+        return remote(block, block, az_s.at[o], az_r.at[o], z_peer((o - near) % 16))
+
+    def amp_half(n):
+        near = 4 if n == 0 else 12
+        h, l = amp_piece(near)
+        block = amp.at[h, l, y, core, pl.ds(16 * n, 16)]
+        return remote(block, block, az_s.at[8 - 8 * n], az_r.at[8 - 8 * n], z_peer(near))
+
+    for o in (1, 15, 2, 14, 4, 12, 3, 13, 5, 11, 6, 10, 7, 9, 8):
+        if o == 8:
+            amp_half(0).wait_recv()
+            amp_half(1).wait_recv()
+        else:
+            amp_z(o).wait_recv()
+        if o == 4:
+            amp_half(0).start()
+            for t in (7, 6, 5):
+                amp_on(t).start()
+        if o == 12:
+            amp_half(1).start()
+            for t in (9, 10, 11):
+                amp_on(t).start()
         for j in (2, 1, 3):
             amp_y(o, j).start()
-
-    for k in (1, 3, 2):
-        int_z(k).wait_recv()
-        for j in (2, 1, 3):
-            int_x(k, j).start()
+        if o == 13:
+            for n in range(2):
+                int_relay(n).wait_recv()
+                int_onward(n).start()
+            for k in (1, 3):
+                int_z(k).wait_recv()
+                for j in (2, 1, 3):
+                    int_x(k, j).start()
+
+    for n in range(2):
+        int_onward(n).wait_recv()
+    for j in (2, 1, 3):
+        int_x(2, j).start()
 
     for j in (1, 2, 3):
         amp_y_own(j).wait_recv()
     amp_c(0).start()
 
-    @pl.loop(1, 16)
-    def _(k):
-        o = ((k // 2) * (1 - 2 * (k % 2)) - (k % 2) + 16) % 16
+    for o in (1, 15, 2, 14, 4, 12, 3, 13, 5, 11, 6, 10, 7, 9, 8):
         for j in (1, 2, 3):
             amp_y(o, j).wait_recv()
         amp_c(o).start()
@@ -267,9 +306,15 @@
     grad_out[0] = s[:, :64].astype(BF16)
     grad_out[1] = s[:, 64:].astype(BF16)
 
+    for o in (1, 2, 3, 4, 5, 6, 7, 9, 10, 11, 12, 13, 14, 15):
+        amp_z(o).wait_send()
+    for n in range(2):
+        amp_half(n).wait_send()
+        int_relay(n).wait_send()
+        int_onward(n).wait_send()
+
     @pl.loop(1, 16)
     def _(o):
-        amp_z(o).wait_send()
         grad_zo(o).wait_send()
 
     @pl.loop(0, 16)
@@ -283,8 +328,9 @@
             int_x(k, j).wait_send()
             grad_yc(k, j).wait_send()
         grad_c(k).wait_send()
+    for k in (1, 3):
+        int_z(k).wait_send()
     for k in (1, 2, 3):
-        int_z(k).wait_send()
         dens_x(k).wait_send()
         dens_z(k).wait_send()
 
@@ -307,6 +353,7 @@
             pltpu.VMEM((8, 128), F32), pltpu.VMEM((2, 32, 64), BF16),
             pltpu.VMEM((2, 64, 2, 128), BF16), pltpu.VMEM((32, 128), BF16),
             pltpu.VMEM((4, 64, 128), BF16), dma((8,)),
+            pltpu.VMEM((2, 32, 128), BF16), dma((2,)), dma((2,)),
             pltpu.VMEM((4, 4, 4, 2, 32, 128), BF16),
             pltpu.VMEM((16, 64, 128), BF16),
             pltpu.VMEM((4, 128, 128), BF16),

time: 59.5 us -> 54.8 us (0.921)
  Pallas kernels: 56.5 us -> 51.6 us
    pallas_call x1, Pallas kernels: 56.5 us -> 51.6 us  [local(): pl.pallas_call(kernel, out_shape=(jax.ShapeDtypeStruct((4, 64, 128), BF16...]
where the time goes in v3:
time: 54.8 us; the launch traced here: 54.4 us
  Pallas kernels  51.6 us (94%)
  local copies, waits for them, and re-layouts  2.15 us (4%)
  between operations  0.65 us (1%)
    pallas_call x1, Pallas kernels, local(): pl.pallas_call(kernel, out_shape=(jax.ShapeDtypeStruct((4, 64, 128), BF16...  51.6 us
    reshape x1, local copies, waits for them, and re-layouts, local(): density = dens.reshape(2, 2, 64, 128).transpose(0, 2, 1, 3)  1.54 us

profile of v3, /device:TPU:1, one launch (start us, length us, event | category | flops | bytes accessed | tf_op | source)
XLA Modules:
  0.0 54.4 jit_solution(10680382219694174658)
XLA Ops:
  0.6 51.6 %shard_map.86 = (bf16[4,64,128]{2,1,0:T(8,128)(2,1)}, bf16[2,32,64]{2,1,0:T(8,128)(2,1)}) custom-call(s32[2]{0:T(128)} %i_list.1, s32[2,2]{1,0:T(2,128)} %pairs.1, s32[2]{0:T(128)} %vir_offsets.1, f32[128]{0:T(128)} %occ_energy.1, f32[1024]{0:T(1024)} %vir_energy.1, f32[8,128]{1,0:T(8,128)} %bitcast.9, bf16[2,32,64]{2,1,0:T(8,128)(2,1)} %bitcast.11, ...), custom_call_target="tpu_custom_call" | custom-call | tf_op jit(solution)/shard_map/pallas_call | solution.py:342
  52.3 0.0 copy-start
  52.3 1.5 %copy.11 = bf16[2,2,64,128]{3,1,2,0:T(2,128)(2,1)} copy(bf16[2,2,64,128]{3,2,1,0:T(8,128)(2,1)} %bitcast.8) | data formatting | bytes 131072 | tf_op jit(solution)/shard_map/reshape | solution.py:380
  53.8 0.0 copy-done
  53.8 0.6 %copy.13 = bf16[2,64,32]{1,2,0:T(8,128)(2,1)} copy(bf16[2,64,32]{1,2,0:T(8,128)(2,1)S(1)} %bitcast.10) | data formatting | bytes 16384
Async XLA Ops:
  52.3 1.6 %copy-start = (bf16[2,32,64]{2,1,0:T(8,128)(2,1)S(1)}, bf16[2,32,64]{2,1,0:T(8,128)(2,1)}, u32[]{:S(2)}) copy-start(bf16[2,32,64]{2,1,0:T(8,128)(2,1)} %get-tuple-element.5) | copy-start | bytes 24580

commit v4 on v3

--- a/solution.py
+++ b/solution.py
@@ -14,10 +14,10 @@
     i_list, pairs, vir_offsets, occ_energy, vir_energy, vir_rows, amp_hbm, int_hbm,
     dens_out, grad_out,
     i_sm, pairs_sm, off_sm, occ_sm, vir_sm, vir_vm, amp_vm, int_vm, amp_in, int_in, in_sem, relay, ir_s, ir_r,
-    amp, ints, scaled, grad, grad_core, grad_y, grad_yrecv, grad_z, grad_zrecv,
-    dens, dens_xrecv, dens_sum, dens_zrecv,
+    amp, ints, ints_t, triples, scaled, grad, grad_core, grad_y, grad_yrecv, grad_z, grad_zrecv,
+    grad_rel, dens, dens_xrecv, dens_sum, dens_zrecv, dens_all,
     az_s, az_r, ay_s, ay_r, ac_s, ac_r, iz_s, iz_r, ix_s, ix_r,
-    dx_s, dx_r, dz_s, dz_r, gc_s, gc_r, gy_s, gy_r, gz_s, gz_r,
+    dx_s, dx_r, dz_s, dz_r, gc_s, gc_r, gy_s, gy_r, gz_s, gz_r, gr_s, gr_r,
 ):
     row = lax.axis_index("row")
     col = lax.axis_index("col")
@@ -203,31 +203,41 @@
     for k in (0, 1, 3, 2):
         for j in (1, 2, 3):
             int_x(k, j).wait_recv()
-    ints_all = ints[...].reshape(1024, 128)
-    ints_t = ints_all.T
-
-    @pl.loop(0, 16)
-    def _(o):
+    for l in range(4):
+        ints_t[l] = ints[4 * l:4 * l + 4].reshape(256, 128).T
+    triples[...] = jnp.zeros_like(triples)
+
+    for o in (0, 1, 15, 2, 14, 4, 12, 3, 13, 5, 11, 6, 10, 7, 9, 8):
         amp_c(o).wait_recv()
-
+        h, l = amp_piece(o)
+        triples[h] += jnp.dot(
+            ints_t[l], amp[h, l].reshape(256, 128), preferred_element_type=F32
+        )
     for h in range(4):
-        t = jnp.dot(ints_t, amp[h].reshape(1024, 128), preferred_element_type=F32)
-        scaled[h] = (t / (row_part[h] - e_a)).astype(BF16)
-
-    def grad_c(h):
-        return remote(
-            grad.at[h, :, :, 1 - core], grad_core.at[h], gc_s.at[h], gc_r.at[h], core_peer
-        )
-
-    for k in (2, 1, 3, 0):
-        h = (zh + k) % 4
-        g = jnp.dot(ints_all, scaled[h], preferred_element_type=F32)
-        grad[h] = g.astype(BF16).reshape(4, 4, 2, 32, 128)
-        grad_c(h).start()
-
-    def dens_x(j):
-        return remote(
-            dens.at[(x + j) % 4], dens_xrecv.at[j], dx_s.at[j], dx_r.at[j], x_peer(j)
+        scaled[h] = (triples[h] / (row_part[h] - e_a)).astype(BF16)
+
+    def grad_c(o):
+        t = (z + o) % 16
+        return remote(
+            grad.at[t, :, 1 - core], grad_core.at[o], gc_s.at[o], gc_r.at[o], core_peer
+        )
+
+    def grad_dot(o):
+        t = (z + o) % 16
+        rows = ints[pl.ds((t % 4) * 4, 4)].reshape(256, 128)
+        g = jnp.dot(rows, scaled[t // 4], preferred_element_type=F32)
+        grad[t] = g.astype(BF16).reshape(4, 2, 32, 128)
+        grad_c(o).start()
+
+    far = (8, 7, 9, 6, 10, 5, 11)
+    near = (3, 13, 2, 14, 1, 15)
+    for o in far:
+        grad_dot(o)
+
+    def dens_x(k, j):
+        return remote(
+            dens.at[(x + j) % 4, (zh + k) % 4], dens_xrecv.at[k, j], dx_s.at[k, j],
+            dx_r.at[k, j], x_peer(j),
         )
 
     for j in (2, 1, 3, 0):
@@ -239,72 +249,113 @@
                 preferred_element_type=F32,
             )
         dens[t] = acc.astype(BF16).reshape(4, 64, 128)
-        if j:
-            dens_x(j).start()
-
-    def grad_yc(k, j):
+    for k in (2, 1, 3, 0):
+        for j in (2, 1, 3):
+            dens_x(k, j).start()
+
+    def grad_yc(o, j):
+        return remote(
+            grad_y.at[o, (y + j) % 4], grad_yrecv.at[o, j], gy_s.at[o, j], gy_r.at[o, j],
+            y_peer(j),
+        )
+
+    def core_sum(o):
+        grad_c(o).wait_recv()
+        v = grad[(z + o) % 16, :, core].astype(F32) + grad_core[o].astype(F32)
+        grad_y[o] = v.astype(BF16)
+        for j in (2, 1, 3):
+            grad_yc(o, j).start()
+
+    for o in far:
+        core_sum(o)
+    for o in (4, 12) + near + (0,):
+        grad_dot(o)
+
+    def dens_z(k):
+        return remote(
+            dens_sum.at[(zh + k) % 4], dens_zrecv.at[k], dz_s.at[k], dz_r.at[k], zh_peer(k)
+        )
+
+    def dens_add(k):
         h = (zh + k) % 4
-        return remote(
-            grad_y.at[h, :, (y + j) % 4], grad_yrecv.at[k, j], gy_s.at[k, j], gy_r.at[k, j],
-            y_peer(j),
-        )
-
-    for k in (2, 1, 3, 0):
-        h = (zh + k) % 4
-        grad_c(h).wait_recv()
-        s = grad[h, :, :, core].astype(F32) + grad_core[h].astype(F32)
-        grad_y[h] = s.astype(BF16)
-        for j in (2, 1, 3):
-            grad_yc(k, j).start()
-
-    def dens_z(k):
-        return remote(
-            dens_sum.at[(zh + k) % 4], dens_zrecv.at[k], dz_s.at[k], dz_r.at[k], zh_peer(k)
-        )
-
-    total = dens[x].astype(F32)
-    for j in (1, 3, 2):
-        dens_x(j).wait_recv()
-        total += dens_xrecv[j].astype(F32)
-    dens_sum[...] = total.astype(BF16)
-    for k in (2, 1, 3):
-        dens_z(k).start()
-
-    def grad_zc(k, m):
-        t = (zl + m) % 4
-        o = (4 * k + t - zl + 16) % 16
-        return remote(
-            grad_z.at[(zh + k) % 4, t], grad_zrecv.at[o], gz_s.at[o], gz_r.at[o], z_peer(o)
-        )
-
-    for k in (2, 1, 3, 0):
-        h = (zh + k) % 4
-        s = grad_y[h, :, y].astype(F32)
+        total = dens[x, h].astype(F32)
         for j in (1, 3, 2):
-            grad_yc(k, j).wait_recv()
-            s += grad_yrecv[k, j].astype(F32)
-        grad_z[h] = s.astype(BF16)
+            dens_x(k, j).wait_recv()
+            total += dens_xrecv[k, j].astype(F32)
+        dens_sum[h] = total.astype(BF16)
+        if k:
+            dens_z(k).start()
+
+    dens_add(2)
+    for o in (4, 12) + near + (0,):
+        core_sum(o)
+    dens_add(1)
+    dens_add(3)
+
+    def y_sum(o):
+        v = grad_y[o, y].astype(F32)
+        for j in (1, 3, 2):
+            grad_yc(o, j).wait_recv()
+            v += grad_yrecv[o, j].astype(F32)
+        return v
+
+    def grad_zc(o):
+        return remote(
+            grad_z.at[o], grad_zrecv.at[o], gz_s.at[o], gz_r.at[o], z_peer(o)
+        )
+
+    def grad_r(n, m):
+        o = 5 + m if n == 0 else 11 - m
+        if m < 3:
+            src, dst = grad_z.at[o], grad_rel.at[n, m]
+        else:
+            half = pl.ds(16 * n, 16)
+            src, dst = grad_z.at[8, half], grad_rel.at[n, 3, half]
+        return remote(
+            src, dst, gr_s.at[n, m], gr_r.at[n, m], z_peer(1 + m if n == 0 else 15 - m)
+        )
+
+    for o in far:
+        grad_z[o] = y_sum(o).astype(BF16)
+        if o == 8:
+            grad_r(0, 3).start()
+            grad_r(1, 3).start()
+        elif o < 8:
+            grad_r(0, o - 5).start()
+        else:
+            grad_r(1, 11 - o).start()
+    dens_add(0)
+    for o in near:
+        grad_z[o] = y_sum(o).astype(BF16)
+        grad_zc(o).start()
+    for n in range(2):
+        o = 4 if n == 0 else 12
+        v = y_sum(o)
         for m in range(4):
-            if k or m:
-                grad_zc(k, m).start()
-
-    dens_out[zh] = dens_sum[zh]
+            grad_r(n, m).wait_recv()
+        for m in range(3):
+            v += grad_rel[n, m].astype(F32)
+        half = slice(16 * n, 16 * n + 16)
+        rest = slice(16 - 16 * n, 32 - 16 * n)
+        grad_z[o, half] = (v[half] + grad_rel[n, 3, half].astype(F32)).astype(BF16)
+        grad_z[o, rest] = v[rest].astype(BF16)
+        grad_zc(o).start()
+    total = y_sum(0)
+
     for k in (1, 3, 2):
         dens_z(k).wait_recv()
-        dens_out[(zh - k + 4) % 4] = dens_zrecv[k]
-
-    def grad_zo(o):
-        return remote(
-            grad_z.at[0, 0], grad_zrecv.at[o], gz_s.at[o], gz_r.at[o], z_peer(o)
-        )
-
-    def add_z(o, s):
-        grad_zo(o).wait_recv()
-        return s + grad_zrecv[o].astype(F32)
-
-    s = lax.fori_loop(1, 16, add_z, grad_z[zh, zl].astype(F32))
-    grad_out[0] = s[:, :64].astype(BF16)
-    grad_out[1] = s[:, 64:].astype(BF16)
+        dens_all[(zh - k + 4) % 4] = dens_zrecv[k]
+    dens_all[zh] = dens_sum[zh]
+    for i in range(2):
+        dens_out[i] = jnp.stack(
+            [dens_all[2 * i].astype(F32), dens_all[2 * i + 1].astype(F32)], axis=1
+        ).astype(BF16)
+
+    for o in near + (4, 12):
+        grad_zc(o).wait_recv()
+        total += grad_zrecv[o].astype(F32)
+    grad_out[0] = total[:, :64].astype(BF16)
+    grad_out[1] = total[:, 64:].astype(BF16)
 
     for o in (1, 2, 3, 4, 5, 6, 7, 9, 10, 11, 12, 13, 14, 15):
         amp_z(o).wait_send()
@@ -313,25 +364,27 @@
         int_relay(n).wait_send()
         int_onward(n).wait_send()
 
-    @pl.loop(1, 16)
-    def _(o):
-        grad_zo(o).wait_send()
+    for o in near + (4, 12):
+        grad_zc(o).wait_send()
+    for n in range(2):
+        for m in range(4):
+            grad_r(n, m).wait_send()
 
     @pl.loop(0, 16)
     def _(o):
         for j in (1, 2, 3):
             amp_y(o, j).wait_send()
+            grad_yc(o, j).wait_send()
         amp_c(o).wait_send()
+        grad_c(o).wait_send()
 
     for k in range(4):
         for j in (1, 2, 3):
             int_x(k, j).wait_send()
-            grad_yc(k, j).wait_send()
-        grad_c(k).wait_send()
+            dens_x(k, j).wait_send()
     for k in (1, 3):
         int_z(k).wait_send()
     for k in (1, 2, 3):
-        dens_x(k).wait_send()
         dens_z(k).wait_send()
 
 
@@ -342,7 +395,7 @@
     dens, grad = pl.pallas_call(
         kernel,
         out_shape=(
-            jax.ShapeDtypeStruct((4, 64, 128), BF16),
+            jax.ShapeDtypeStruct((2, 64, 2, 128), BF16),
             jax.ShapeDtypeStruct((2, 32, 64), BF16),
         ),
         in_specs=[hbm] * 8,
@@ -356,29 +409,33 @@
             pltpu.VMEM((2, 32, 128), BF16), dma((2,)), dma((2,)),
             pltpu.VMEM((4, 4, 4, 2, 32, 128), BF16),
             pltpu.VMEM((16, 64, 128), BF16),
+            pltpu.VMEM((4, 128, 256), BF16),
+            pltpu.VMEM((4, 128, 128), F32),
             pltpu.VMEM((4, 128, 128), BF16),
-            pltpu.VMEM((4, 4, 4, 2, 32, 128), BF16),
-            pltpu.VMEM((4, 4, 4, 32, 128), BF16),
-            pltpu.VMEM((4, 4, 4, 32, 128), BF16),
-            pltpu.VMEM((4, 4, 4, 32, 128), BF16),
-            pltpu.VMEM((4, 4, 32, 128), BF16),
+            pltpu.VMEM((16, 4, 2, 32, 128), BF16),
+            pltpu.VMEM((16, 4, 32, 128), BF16),
+            pltpu.VMEM((16, 4, 32, 128), BF16),
+            pltpu.VMEM((16, 4, 32, 128), BF16),
             pltpu.VMEM((16, 32, 128), BF16),
+            pltpu.VMEM((16, 32, 128), BF16),
+            pltpu.VMEM((2, 4, 32, 128), BF16),
             pltpu.VMEM((4, 4, 64, 128), BF16),
             pltpu.VMEM((4, 4, 64, 128), BF16),
             pltpu.VMEM((4, 64, 128), BF16),
             pltpu.VMEM((4, 64, 128), BF16),
+            pltpu.VMEM((4, 64, 128), BF16),
             dma((16,)), dma((16,)), dma((16, 4)), dma((16, 4)), dma((16,)), dma((16,)),
             dma((4,)), dma((4,)), dma((4, 4)), dma((4, 4)),
-            dma((4,)), dma((4,)), dma((4,)), dma((4,)),
-            dma((4,)), dma((4,)), dma((4, 4)), dma((4, 4)), dma((16,)), dma((16,)),
+            dma((4, 4)), dma((4, 4)), dma((4,)), dma((4,)),
+            dma((16,)), dma((16,)), dma((16, 4)), dma((16, 4)), dma((16,)), dma((16,)),
+            dma((2, 4)), dma((2, 4)),
         ],
         compiler_params=pltpu.CompilerParams(collective_id=0, has_side_effects=True),
     )(
         i_list, pairs, vir_offsets, occ_energy, vir_energy, vir_energy.reshape(8, 128),
         amplitudes.transpose(0, 2, 1), integrals,
     )
-    density = dens.reshape(2, 2, 64, 128).transpose(0, 2, 1, 3)
-    return density, grad.transpose(0, 2, 1)
+    return dens, grad.transpose(0, 2, 1)
 
 
 def solution(mesh):

time: 54.8 us -> 55.6 us (1.015)
  the two profiles are of different devices: /device:TPU:1 before, /device:TPU:24 now
where the time goes in v4:
time: 55.6 us; the launch traced here: 55.4 us
  Pallas kernels  52.7 us (95%)
  local copies, waits for them, and re-layouts  2.13 us (4%)
  between operations  0.65 us (1%)
    pallas_call x1, Pallas kernels, local(): pl.pallas_call(kernel, out_shape=(jax.ShapeDtypeStruct((2, 64, 2, 128), B...  52.7 us
    unnamed x4, local copies, waits for them, and re-layouts  2.13 us

profile of v4, /device:TPU:24, one launch (start us, length us, event | category | flops | bytes accessed | tf_op | source)
XLA Modules:
  0.0 55.4 jit_solution(5689562537931553479)
XLA Ops:
  0.6 52.7 %shard_map.86 = (bf16[2,64,2,128]{3,2,1,0:T(2,128)(2,1)}, bf16[2,32,64]{2,1,0:T(8,128)(2,1)}) custom-call(s32[2]{0:T(128)} %i_list.1, s32[2,2]{1,0:T(2,128)} %pairs.1, s32[2]{0:T(128)} %vir_offsets.1, f32[128]{0:T(128)} %occ_energy.1, f32[1024]{0:T(1024)} %vir_energy.1, f32[8,128]{1,0:T(8,128)} %bitcast.3, bf16[2,32,64]{2,1,0:T(8,128)(2,1)} %bitcast.5, ...), custom_call_target="tpu_custom_call" | custom-call | tf_op jit(solution)/shard_map/pallas_call | solution.py:395
  53.3 0.0 copy-start
  53.3 1.5 %copy.11 = bf16[2,64,2,128]{3,2,1,0:T(2,128)(2,1)} copy(bf16[2,64,2,128]{3,2,1,0:T(2,128)(2,1)} %get-tuple-element.8) | data formatting | bytes 131072
  54.8 0.0 copy-done
  54.8 0.6 %copy.12 = bf16[2,64,32]{1,2,0:T(8,128)(2,1)} copy(bf16[2,64,32]{1,2,0:T(8,128)(2,1)S(1)} %bitcast.4) | data formatting | bytes 16384
Async XLA Ops:
  53.3 1.5 %copy-start = (bf16[2,32,64]{2,1,0:T(8,128)(2,1)S(1)}, bf16[2,32,64]{2,1,0:T(8,128)(2,1)}, u32[]{:S(2)}) copy-start(bf16[2,32,64]{2,1,0:T(8,128)(2,1)} %get-tuple-element.5) | copy-start | bytes 24580

commit v5 on v3

--- a/solution.py
+++ b/solution.py
@@ -214,20 +214,10 @@
         t = jnp.dot(ints_t, amp[h].reshape(1024, 128), preferred_element_type=F32)
         scaled[h] = (t / (row_part[h] - e_a)).astype(BF16)
 
-    def grad_c(h):
-        return remote(
-            grad.at[h, :, :, 1 - core], grad_core.at[h], gc_s.at[h], gc_r.at[h], core_peer
-        )
-
-    for k in (2, 1, 3, 0):
-        h = (zh + k) % 4
-        g = jnp.dot(ints_all, scaled[h], preferred_element_type=F32)
-        grad[h] = g.astype(BF16).reshape(4, 4, 2, 32, 128)
-        grad_c(h).start()
-
-    def dens_x(j):
-        return remote(
-            dens.at[(x + j) % 4], dens_xrecv.at[j], dx_s.at[j], dx_r.at[j], x_peer(j)
+    def dens_x(k, j):
+        return remote(
+            dens.at[(x + j) % 4, (zh + k) % 4], dens_xrecv.at[k, j], dx_s.at[k, j],
+            dx_r.at[k, j], x_peer(j),
         )
 
     for j in (2, 1, 3, 0):
@@ -239,8 +229,35 @@
                 preferred_element_type=F32,
             )
         dens[t] = acc.astype(BF16).reshape(4, 64, 128)
-        if j:
-            dens_x(j).start()
+    for k in (2, 1, 3, 0):
+        for j in (2, 1, 3):
+            dens_x(k, j).start()
+
+    def grad_c(h):
+        return remote(
+            grad.at[h, :, :, 1 - core], grad_core.at[h], gc_s.at[h], gc_r.at[h], core_peer
+        )
+
+    for k in (2, 1, 3, 0):
+        h = (zh + k) % 4
+        g = jnp.dot(ints_all, scaled[h], preferred_element_type=F32)
+        grad[h] = g.astype(BF16).reshape(4, 4, 2, 32, 128)
+        grad_c(h).start()
+
+    def dens_z(k):
+        return remote(
+            dens_sum.at[(zh + k) % 4], dens_zrecv.at[k], dz_s.at[k], dz_r.at[k], zh_peer(k)
+        )
+
+    def dens_add(k):
+        h = (zh + k) % 4
+        total = dens[x, h].astype(F32)
+        for j in (1, 3, 2):
+            dens_x(k, j).wait_recv()
+            total += dens_xrecv[k, j].astype(F32)
+        dens_sum[h] = total.astype(BF16)
+        if k:
+            dens_z(k).start()
 
     def grad_yc(k, j):
         h = (zh + k) % 4
@@ -257,18 +274,8 @@
         for j in (2, 1, 3):
             grad_yc(k, j).start()
 
-    def dens_z(k):
-        return remote(
-            dens_sum.at[(zh + k) % 4], dens_zrecv.at[k], dz_s.at[k], dz_r.at[k], zh_peer(k)
-        )
-
-    total = dens[x].astype(F32)
-    for j in (1, 3, 2):
-        dens_x(j).wait_recv()
-        total += dens_xrecv[j].astype(F32)
-    dens_sum[...] = total.astype(BF16)
-    for k in (2, 1, 3):
-        dens_z(k).start()
+    for k in (2, 1, 3, 0):
+        dens_add(k)
 
     def grad_zc(k, m):
         t = (zl + m) % 4
@@ -327,11 +334,11 @@
         for j in (1, 2, 3):
             int_x(k, j).wait_send()
             grad_yc(k, j).wait_send()
+            dens_x(k, j).wait_send()
         grad_c(k).wait_send()
     for k in (1, 3):
         int_z(k).wait_send()
     for k in (1, 2, 3):
-        dens_x(k).wait_send()
         dens_z(k).wait_send()
 
 
@@ -369,13 +376,18 @@
             pltpu.VMEM((4, 64, 128), BF16),
             dma((16,)), dma((16,)), dma((16, 4)), dma((16, 4)), dma((16,)), dma((16,)),
             dma((4,)), dma((4,)), dma((4, 4)), dma((4, 4)),
-            dma((4,)), dma((4,)), dma((4,)), dma((4,)),
+            dma((4, 4)), dma((4, 4)), dma((4,)), dma((4,)),
             dma((4,)), dma((4,)), dma((4, 4)), dma((4, 4)), dma((16,)), dma((16,)),
         ],
-        compiler_params=pltpu.CompilerParams(collective_id=0, has_side_effects=True),
+        compiler_params=pltpu.CompilerParams(collective_id=0, has_side_effects=True, vmem_limit_bytes=24 << 20),
     )(
-        i_list, pairs, vir_offsets, occ_energy, vir_energy, vir_energy.reshape(8, 128),
-        amplitudes.transpose(0, 2, 1), integrals,
+        *(
+            pltpu.with_memory_space_constraint(v, pltpu.HBM)
+            for v in (
+                i_list, pairs, vir_offsets, occ_energy, vir_energy, vir_energy.reshape(8, 128),
+                amplitudes.transpose(0, 2, 1), integrals,
+            )
+        )
     )
     density = dens.reshape(2, 2, 64, 128).transpose(0, 2, 1, 3)
     return density, grad.transpose(0, 2, 1)

time: 54.8 us -> 53.1 us (0.969)
  local copies, waits for them, and re-layouts: 2.15 us -> 1.3 us
  Pallas kernels: 51.6 us -> 51 us
    reshape x1, local copies, waits for them, and re-layouts: 1.54 us -> 0.7 us  [local(): density = dens.reshape(2, 2, 64, 128).transpose(0, 2, 1, 3)]
    pallas_call x1, Pallas kernels: 51.6 us -> 51 us  [local(): pl.pallas_call(kernel, out_shape=(jax.ShapeDtypeStruct((4, 64, 128), BF16...]
where the time goes in v5:
time: 53.1 us; the launch traced here: 52.9 us
  Pallas kernels  51 us (96%)
  local copies, waits for them, and re-layouts  1.3 us (2%)
  between operations  0.64 us (1%)
    pallas_call x1, Pallas kernels, local(): pl.pallas_call(kernel, out_shape=(jax.ShapeDtypeStruct((4, 64, 128), BF16...  51 us

profile of v5, /device:TPU:1, one launch (start us, length us, event | category | flops | bytes accessed | tf_op | source)
XLA Modules:
  0.0 52.9 jit_solution(3241160982101655997)
XLA Ops:
  0.6 51.0 %shard_map.86 = (bf16[4,64,128]{2,1,0:T(8,128)(2,1)S(1)}, bf16[2,32,64]{2,1,0:T(8,128)(2,1)S(1)}) custom-call(s32[2]{0:T(128)} %i_list.1, s32[2,2]{1,0:T(2,128)} %pairs.1, s32[2]{0:T(128)} %vir_offsets.1, f32[128]{0:T(128)} %occ_energy.1, f32[1024]{0:T(1024)} %vir_energy.1, f32[8,128]{1,0:T(8,128)} %bitcast.10, bf16[2,32,64]{2,1,0:T(8,128)(2,1)} %bitcast.11, ...), custom_call_target="tpu_custom_call" | custom-call | tf_op jit(solution)/shard_map/pallas_call | solution.py:349
  51.6 0.7 %copy.11 = bf16[2,2,64,128]{3,1,2,0:T(2,128)(2,1)} copy(bf16[2,2,64,128]{3,2,1,0:T(8,128)(2,1)S(1)} %bitcast.7) | data formatting | bytes 131072 | tf_op jit(solution)/shard_map/reshape | solution.py:392
  52.3 0.6 %copy.13 = bf16[2,64,32]{1,2,0:T(8,128)(2,1)} copy(bf16[2,64,32]{1,2,0:T(8,128)(2,1)S(1)} %bitcast.8) | data formatting | bytes 16384

commit v6 on v5

--- a/solution.py
+++ b/solution.py
@@ -53,20 +53,20 @@
             (pairs, pairs_sm), (vir_offsets, off_sm), (occ_energy, occ_sm), (vir_energy, vir_sm),
         ))
     ]
-    for load in loads:
-        load.start()
-
     barrier = pltpu.get_barrier_semaphore()
 
     def greet(dev):
         pl.semaphore_signal(barrier, inc=1, device_id=dev, device_id_type=MESH)
 
-    for o in (1, 2, 3, 4, 12, 13, 14, 15):
+    loads[0].start()
+    for o in (4, 12, 3, 13, 2, 14, 1, 15):
         greet(z_peer(o))
     for j in range(1, 4):
         greet(x_peer(j))
         greet(y_peer(j))
     greet(core_peer)
+    for load in loads[1:]:
+        load.start()
     loads[0].wait()
     amp_in[...] = jnp.concatenate([amp_vm[0], amp_vm[1]], axis=1)
     amp[zh, zl, y, core] = amp_in[...]
@@ -214,6 +214,19 @@
         t = jnp.dot(ints_t, amp[h].reshape(1024, 128), preferred_element_type=F32)
         scaled[h] = (t / (row_part[h] - e_a)).astype(BF16)
 
+    def grad_c(h):
+        return remote(
+            grad.at[h, :, :, 1 - core], grad_core.at[h], gc_s.at[h], gc_r.at[h], core_peer
+        )
+
+    def grad_dot(k):
+        h = (zh + k) % 4
+        g = jnp.dot(ints_all, scaled[h], preferred_element_type=F32)
+        grad[h] = g.astype(BF16).reshape(4, 4, 2, 32, 128)
+        grad_c(h).start()
+
+    grad_dot(2)
+
     def dens_x(k, j):
         return remote(
             dens.at[(x + j) % 4, (zh + k) % 4], dens_xrecv.at[k, j], dx_s.at[k, j],
@@ -233,16 +246,8 @@
         for j in (2, 1, 3):
             dens_x(k, j).start()
 
-    def grad_c(h):
-        return remote(
-            grad.at[h, :, :, 1 - core], grad_core.at[h], gc_s.at[h], gc_r.at[h], core_peer
-        )
-
-    for k in (2, 1, 3, 0):
-        h = (zh + k) % 4
-        g = jnp.dot(ints_all, scaled[h], preferred_element_type=F32)
-        grad[h] = g.astype(BF16).reshape(4, 4, 2, 32, 128)
-        grad_c(h).start()
+    for k in (1, 3, 0):
+        grad_dot(k)
 
     def dens_z(k):
         return remote(
@@ -273,9 +278,8 @@
         grad_y[h] = s.astype(BF16)
         for j in (2, 1, 3):
             grad_yc(k, j).start()
-
-    for k in (2, 1, 3, 0):
-        dens_add(k)
+        if k in (1, 3):
+            dens_add(2 if k == 1 else 1)
 
     def grad_zc(k, m):
         t = (zl + m) % 4
@@ -294,6 +298,9 @@
         for m in range(4):
             if k or m:
                 grad_zc(k, m).start()
+        if k == 2:
+            dens_add(3)
+            dens_add(0)
 
     dens_out[zh] = dens_sum[zh]
     for k in (1, 3, 2):

time: 53.1 us -> 51.8 us (0.976)
  Pallas kernels: 51 us -> 49.7 us
    pallas_call x1, Pallas kernels: 51 us -> 49.7 us  [local(): pl.pallas_call(kernel, out_shape=(jax.ShapeDtypeStruct((4, 64, 128), BF16...]
where the time goes in v6:
time: 51.8 us; the launch traced here: 51.6 us
  Pallas kernels  49.7 us (96%)
  local copies, waits for them, and re-layouts  1.3 us (3%)
  between operations  0.64 us (1%)
    pallas_call x1, Pallas kernels, local(): pl.pallas_call(kernel, out_shape=(jax.ShapeDtypeStruct((4, 64, 128), BF16...  49.7 us

profile of v6, /device:TPU:1, one launch (start us, length us, event | category | flops | bytes accessed | tf_op | source)
XLA Modules:
  0.0 51.6 jit_solution(2789063521987783036)
XLA Ops:
  0.6 49.7 %shard_map.86 = (bf16[4,64,128]{2,1,0:T(8,128)(2,1)S(1)}, bf16[2,32,64]{2,1,0:T(8,128)(2,1)S(1)}) custom-call(s32[2]{0:T(128)} %i_list.1, s32[2,2]{1,0:T(2,128)} %pairs.1, s32[2]{0:T(128)} %vir_offsets.1, f32[128]{0:T(128)} %occ_energy.1, f32[1024]{0:T(1024)} %vir_energy.1, f32[8,128]{1,0:T(8,128)} %bitcast.10, bf16[2,32,64]{2,1,0:T(8,128)(2,1)} %bitcast.11, ...), custom_call_target="tpu_custom_call" | custom-call | tf_op jit(solution)/shard_map/pallas_call | solution.py:356
  50.3 0.7 %copy.11 = bf16[2,2,64,128]{3,1,2,0:T(2,128)(2,1)} copy(bf16[2,2,64,128]{3,2,1,0:T(8,128)(2,1)S(1)} %bitcast.7) | data formatting | bytes 131072 | tf_op jit(solution)/shard_map/reshape | solution.py:399
  51.0 0.6 %copy.13 = bf16[2,64,32]{1,2,0:T(8,128)(2,1)} copy(bf16[2,64,32]{1,2,0:T(8,128)(2,1)S(1)} %bitcast.8) | data formatting | bytes 16384
